TPU v7x, 256 devices: a whole 4x4x8 slice. The times are simulated.
256 devices in a mesh: dp: 16 (over y_hi, x, core), tensor: 16 (over z, y_lo).
Axes of the slice: x: 4, y: 4 (y_hi: 2, y_lo: 2; y = y_hi * 2 + y_lo), z: 8, core: 2. Of those that a mesh axis runs over, the one named last changes fastest.
Arguments:
- tokens: bfloat16 [8192, 8192], P('dp', 'tensor'), may hold values from -13 to 13
- proj: bfloat16 [8192, 8192], P('tensor'), may hold values from -8 to 8
- gain: float32 [8192], P('tensor'), may hold values from 0.1 to 1.9
- target: bfloat16 [8192, 8192], P('dp', 'tensor'), may hold values from -6 to 6
- adapter_down_weight: bfloat16 [256, 64, 8192], P('dp', None, 'tensor'), may hold values from -0.0625 to 0.0625
- adapter_up_weight: bfloat16 [256, 64, 8192], P('dp', None, 'tensor'), may hold values from -0.75 to 0.75
- source_row_index: int32 [16, 16, 96], P('dp'), may hold values from 0 to 512, as said below
- padded_row_index: int32 [16, 3584], P('dp'), may hold values from 0 to 1536, as said below
- padded_block_tenant: int32 [16, 28], P('dp'), may hold values from 0 to 15, as said below
Outputs:
- draft: bfloat16 [8192, 8192], P('dp', 'tensor')
- grad_down: bfloat16 [256, 64, 8192], P('dp', None, 'tensor')
- grad_up: bfloat16 [256, 64, 8192], P('dp', None, 'tensor')
Inputs may be any that keep to these rules, and one draw needn't show every extreme that they name: For source s and owner d, the first c[s, d] entries of source_row_index[s, d] are rows of source s and the rest are 512; every row of a source appears exactly once over all owners. Some source fills all 96 slots to some owner, and some owner receives 96 rows from every source. `padded_row_index`: for owner d, every live slot s * 96 + j (source_row_index[s, d, j] < 512) appears exactly once, all other entries are 1536; the rows of one block of 128 padded rows belong to one tenant. `padded_block_tenant`: nondecreasing along the blocks of an owner.
All inputs are finite; a program needn't handle non-finite values.
Results may differ from a plain program's by a relative error of at most 0.02.
Values may be sent and summed in bfloat16 or wider, within the bound.
A program may use at most 128 MiB of HBM per device.

v0:
```python
import jax
import jax.numpy as jnp
from jax import lax
from jax.sharding import PartitionSpec as P

MODEL_WIDTH = 8192


def to_padded(values, positions):
    extended = jnp.concatenate([values, jnp.zeros((1, values.shape[1]), values.dtype)])
    return extended[positions]


def body(
    tokens,
    proj,
    gain,
    target,
    adapter_down_weight,
    adapter_up_weight,
    source_row_index,
    padded_row_index,
    padded_block_tenant,
):
    row_count, feat_width = tokens.shape
    dp_count = lax.axis_size("dp")
    slot_cap = source_row_index.shape[2]
    slot_total = dp_count * slot_cap
    routes = source_row_index[0].reshape(slot_total)
    positions = padded_row_index[0]
    local_tenant_index = padded_block_tenant[0]
    block_count = local_tenant_index.shape[0]
    block_rows = positions.shape[0] // block_count
    outgoing = to_padded(tokens, routes).reshape(dp_count, slot_cap, feat_width)
    arrived = lax.all_to_all(outgoing, "dp", split_axis=0, concat_axis=0, tiled=True)
    feat_padded = to_padded(arrived.reshape(slot_total, feat_width), positions).reshape(
        block_count, block_rows, feat_width
    )
    down_weight_tiles = adapter_down_weight[local_tenant_index]
    up_weight_tiles = adapter_up_weight[local_tenant_index]
    rank_part = jnp.einsum(
        "brk,bpk->brp", down_weight_tiles, feat_padded, preferred_element_type=jnp.float32
    )
    rank_act = lax.psum(rank_part.astype(jnp.bfloat16), "tensor")
    delta_pad = (
        2.0
        * jnp.einsum("brp,bro->bpo", rank_act, up_weight_tiles, preferred_element_type=jnp.float32)
    ).astype(jnp.bfloat16)
    delta_slots = (
        jnp.zeros((slot_total + 1, feat_width), jnp.bfloat16)
        .at[positions]
        .set(delta_pad.reshape(-1, feat_width))[:slot_total]
    )
    returned = lax.all_to_all(
        delta_slots.reshape(dp_count, slot_cap, feat_width),
        "dp",
        split_axis=0,
        concat_axis=0,
        tiled=True,
    )
    delta_rows = (
        jnp.zeros((row_count + 1, feat_width), jnp.bfloat16)
        .at[routes]
        .set(returned.reshape(slot_total, feat_width))[:row_count]
    )
    col_start = lax.axis_index("tensor") * feat_width
    partial_value = jnp.dot(tokens, proj, preferred_element_type=jnp.float32)
    own_cols = lax.dynamic_slice_in_dim(
        partial_value, col_start, feat_width, 1
    ) + delta_rows.astype(jnp.float32)
    partial_value = lax.dynamic_update_slice_in_dim(partial_value, own_cols, col_start, 1)
    hidden = lax.psum_scatter(
        partial_value.astype(jnp.bfloat16), "tensor", scatter_dimension=1, tiled=True
    ).astype(jnp.float32)
    square_total = lax.psum(jnp.sum(hidden * hidden, axis=1), "tensor")
    inv_rms = lax.rsqrt(square_total / MODEL_WIDTH + 1e-05)[:, None]
    scaled = hidden * inv_rms
    gain_row = gain[None, :]
    normed = scaled * gain_row
    draft = normed.astype(jnp.bfloat16)
    weighted = gain_row * ((normed - target.astype(jnp.float32)) / 8.0)
    grad_total = lax.psum(jnp.sum(weighted * scaled, axis=1), "tensor")
    grad_hidden = (inv_rms * (weighted - scaled * (grad_total / MODEL_WIDTH)[:, None])).astype(
        jnp.bfloat16
    )
    grad_send = to_padded(grad_hidden, routes).reshape(dp_count, slot_cap, feat_width)
    grad_arrived = lax.all_to_all(grad_send, "dp", split_axis=0, concat_axis=0, tiled=True)
    grad_padded = to_padded(grad_arrived.reshape(slot_total, feat_width), positions).reshape(
        block_count, block_rows, feat_width
    )
    onehot = (
        local_tenant_index[:, None]
        == jnp.arange(adapter_down_weight.shape[0], dtype=jnp.int32)[None, :]
    ).astype(jnp.float32)
    up_part = 2.0 * jnp.einsum(
        "brp,bpo->bro", rank_act, grad_padded, preferred_element_type=jnp.float32
    )
    grad_up = jnp.einsum("bt,bro->tro", onehot, up_part, precision=lax.Precision.HIGHEST).astype(
        jnp.bfloat16
    )
    back_part = 2.0 * jnp.einsum(
        "bpo,bro->brp", grad_padded, up_weight_tiles, preferred_element_type=jnp.float32
    )
    back_act = lax.psum(back_part.astype(jnp.bfloat16), "tensor")
    down_part = jnp.einsum(
        "brp,bpk->brk", back_act, feat_padded, preferred_element_type=jnp.float32
    )
    grad_down = jnp.einsum(
        "bt,brk->trk", onehot, down_part, precision=lax.Precision.HIGHEST
    ).astype(jnp.bfloat16)
    return (draft, grad_down, grad_up)


def solution(mesh):
    return jax.shard_map(
        body,
        mesh=mesh,
        in_specs=(
            P("dp", "tensor"),
            P("tensor", None),
            P("tensor"),
            P("dp", "tensor"),
            P("dp", None, "tensor"),
            P("dp", None, "tensor"),
            P("dp", None, None),
            P("dp", None),
            P("dp", None),
        ),
        out_specs=(P("dp", "tensor"), P("dp", None, "tensor"), P("dp", None, "tensor")),
        check_vma=False,
    )
```

profile of v0, /device:TPU:2, one launch (start us, length us, event | category | flops | bytes accessed | tf_op | source)
XLA Modules:
  0.0 718.3 jit_solution(15485561268796979615)
XLA Ops:
  9.2 5.4 gather_fusion.1
  14.6 7.6 %all-to-all-start = ((bf16[16,96,512]{2,1,0:T(8,128)(2,1)}), bf16[16,96,512]{2,1,0:T(8,128)(2,1)S(1)}, u32[]{:S(2)}, u32[]{:S(2)}) async-start(bf16[16,96,512]{2,1,0:T(8,128)(2,1)} %bitcast.3), calls=%async_computation | async-start | bytes 3145728 | tf_op jit(solution)/shard_map/all_to_all | solution.py:35
  24.3 19.2 %all-to-all-done = bf16[16,96,512]{2,1,0:T(8,128)(2,1)S(1)} async-done(((bf16[16,96,512]{2,1,0:T(8,128)(2,1)}), bf16[16,96,512]{2,1,0:T(8,128)(2,1)S(1)}, u32[]{:S(2)}, u32[]{:S(2)}) %all-to-all-start) | async-done | bytes 1572896 | tf_op jit(solution)/shard_map/all_to_all | solution.py:35
  46.2 11.0 %gather_fusion.2 = bf16[3584,512]{1,0:T(8,128)(2,1)} fusion(bf16[1537,512]{1,0:T(8,128)(2,1)S(1)} %concatenate.13, s32[4096]{0:T(1024)S(1)} %pad_clamp_fusion), kind=kCustom, calls=%fused_computation.2 | custom fusion | bytes 7354368 | tf_op jit(solution)/shard_map/gather | solution.py:11
  57.2 4.8 convolution_convert_fusion
  62.7 137.0 %all-reduce.7.cloned.1.call-done = bf16[28,64,128]{2,1,0:T(8,128)(2,1)} async-done(((bf16[28,64,128]{2,1,0:T(8,128)(2,1)}), bf16[28,64,128]{2,1,0:T(8,128)(2,1)}) %all-reduce.7.cloned.1.call-update) | async-done | bytes 458768 | tf_op jit(solution)/shard_map/psum | solution.py:44
  199.7 4.0 multiply_convert_fusion
  203.7 17.7 %scatter_custom_fusion = bf16[1537,512]{1,0:T(8,128)(2,1)} fusion(s32[3584]{0:T(1024)S(1)} %fusion.24, bf16[3584,512]{1,0:T(8,128)(2,1)} %bitcast.40, bf16[]{:T(256)} %constant.17.clone.1), kind=kCustom, calls=%fused_computation.33 | custom fusion | bytes 1574400 | tf_op jit(solution)/shard_map/scatter | solution.py:52
  224.1 7.2 %all-to-all-start.1 = ((bf16[16,96,512]{2,1,0:T(8,128)(2,1)}), bf16[16,96,512]{2,1,0:T(8,128)(2,1)S(1)}, u32[]{:S(2)}, u32[]{:S(2)}) async-start(bf16[16,96,512]{2,1,0:T(8,128)(2,1)} %bitcast.36), calls=%async_computation.1 | async-start | bytes 3145728 | tf_op jit(solution)/shard_map/all_to_all | solution.py:54
  231.5 11.5 %fusion.33 = f32[512,8192]{1,0:T(8,128)} fusion(bf16[512,512]{1,0:T(8,128)(2,1)S(1)} %copy-done.4, bf16[512,8192]{1,0:T(8,128)(2,1)} %param.10), kind=kOutput, calls=%fused_computation.54 | convolution fusion | flops 4294967296 | bytes 25690112 | tf_op jit(solution)/shard_map/dot_general | solution.py:67
  243.0 9.6 %all-to-all-done.1 = bf16[16,96,512]{2,1,0:T(8,128)(2,1)S(1)} async-done(((bf16[16,96,512]{2,1,0:T(8,128)(2,1)}), bf16[16,96,512]{2,1,0:T(8,128)(2,1)S(1)}, u32[]{:S(2)}, u32[]{:S(2)}) %all-to-all-start.1) | async-done | bytes 1572896 | tf_op jit(solution)/shard_map/all_to_all | solution.py:54
  252.6 7.3 %scatter_custom_fusion.1 = bf16[513,512]{1,0:T(8,128)(2,1)S(1)} fusion(s32[1536]{0:T(1024)S(1)} %fusion.28, bf16[1536,512]{1,0:T(8,128)(2,1)S(1)} %bitcast.41, bf16[]{:T(256)} %constant.17.clone.1), kind=kCustom, calls=%fused_computation.35 | custom fusion | bytes 525314 | tf_op jit(solution)/shard_map/scatter | solution.py:64
  262.3 8.9 %convert_element_type.37 = bf16[512,8192]{1,0:T(8,128)(2,1)} convert(f32[512,8192]{1,0:T(8,128)} %add_dynamic-update-slice_fusion) | non-fusion elementwise | flops 4194304 | bytes 25165824 | tf_op jit(solution)/shard_map/convert_element_type | solution.py:73
  271.9 179.6 %reduce-scatter.2.cloned.1.call-done = bf16[512,512]{1,0:T(8,128)(2,1)} async-done(((bf16[512,8192]{1,0:T(8,128)(2,1)}), bf16[512,512]{1,0:T(8,128)(2,1)}) %reduce-scatter.2.cloned.1.call-update) | async-done | bytes 524304 | tf_op jit(solution)/shard_map/reduce_scatter | solution.py:72
  452.8 33.3 %psum.29 = f32[512]{0:T(512)S(1)} all-reduce(f32[512]{0:T(512)S(1)} %fusion.19), channel_id=1, replica_groups=mesh['dp'=16,'tensor'=16] {'tensor'}, use_global_device_ids=true, to_apply=%region_5.0 | all-reduce | flops 512 | bytes 4096 | tf_op jit(solution)/shard_map/psum | solution.py:75
  487.6 30.6 %psum.30 = f32[512]{0:T(512)S(1)} all-reduce(f32[512]{0:T(512)S(1)} %fusion.15), channel_id=1, replica_groups=mesh['dp'=16,'tensor'=16] {'tensor'}, use_global_device_ids=true, to_apply=%region_7.0 | all-reduce | flops 512 | bytes 4096 | tf_op jit(solution)/shard_map/psum | solution.py:82
  520.5 4.8 gather_fusion.4
  525.3 27.0 %all_to_all.15 = bf16[16,96,512]{2,1,0:T(8,128)(2,1)S(1)} all-to-all(bf16[16,96,512]{2,1,0:T(8,128)(2,1)S(1)} %bitcast.37), channel_id=1, replica_groups=mesh['dp'=16,'tensor'=16] {'dp'}, dimensions={0} | all-to-all | bytes 3145728 | tf_op jit(solution)/shard_map/all_to_all | solution.py:87
  552.4 11.0 %gather_fusion.5 = bf16[3584,512]{1,0:T(8,128)(2,1)} fusion(bf16[1537,512]{1,0:T(8,128)(2,1)S(1)} %concatenate.15, s32[4096]{0:T(1024)S(1)} %pad_clamp_fusion), kind=kCustom, calls=%fused_computation.5 | custom fusion | bytes 7354368 | tf_op jit(solution)/shard_map/gather | solution.py:11
  563.4 4.8 fusion.11
  570.9 3.7 fusion.7
  576.2 127.6 %all-reduce.9.cloned.1.call-done = bf16[28,64,128]{2,1,0:T(8,128)(2,1)} async-done(((bf16[28,64,128]{2,1,0:T(8,128)(2,1)}), bf16[28,64,128]{2,1,0:T(8,128)(2,1)}) %all-reduce.9.cloned.1.call-update) | async-done | bytes 458768 | tf_op jit(solution)/shard_map/psum | solution.py:104
  703.7 2.9 fusion.34
  706.7 3.6 fusion.4
  (52 shorter events, 24.2 us)
Async XLA Ops:
  7.2 15.2 %copy-start = (bf16[16,64,512]{2,1,0:T(8,128)(2,1)S(1)}, bf16[16,64,512]{2,1,0:T(8,128)(2,1)}, u32[]{:S(2)}) copy-start(bf16[16,64,512]{2,1,0:T(8,128)(2,1)} %param.13) | copy-start | bytes 3145732
  9.2 13.1 %copy-start.10 = (s32[1,28]{1,0:T(1,128)S(1)}, s32[1,28]{1,0:T(1,128)}, u32[]{:S(2)}) copy-start(s32[1,28]{1,0:T(1,128)} %param.17) | copy-start | bytes 340
  14.6 9.7 %copy-start.9 = (s32[1,3584]{1,0:T(1,128)S(1)}, s32[1,3584]{1,0:T(1,128)}, u32[]{:S(2)}) copy-start(s32[1,3584]{1,0:T(1,128)} %param.16) | copy-start | bytes 43012
  14.6 28.9 %all-to-all-start = ((bf16[16,96,512]{2,1,0:T(8,128)(2,1)}), bf16[16,96,512]{2,1,0:T(8,128)(2,1)S(1)}, u32[]{:S(2)}, u32[]{:S(2)}) async-start(bf16[16,96,512]{2,1,0:T(8,128)(2,1)} %bitcast.3), calls=%async_computation | async-start | bytes 3145728 | tf_op jit(solution)/shard_map/all_to_all | solution.py:35
  22.2 177.5 %all-reduce.7.cloned.1.call-start = ((), (), s32[]{:S(2)}) async-start(), calls=%async_computation.4 | async-start | bytes 917504 | tf_op jit(solution)/shard_map/psum | solution.py:44
  43.5 1.1 copy-start.3
  57.2 4.8 copy-start.5
  62.7 158.7 %copy-start.2 = (bf16[28,64,512]{2,1,0:T(8,128)(2,1)}, bf16[28,64,512]{2,1,0:T(8,128)(2,1)S(1)}, u32[]{:S(2)}) copy-start(bf16[28,64,512]{2,1,0:T(8,128)(2,1)S(1)} %gather_fusion.3) | copy-start | bytes 5505028
  203.7 27.8 %copy-start.4 = (bf16[512,512]{1,0:T(8,128)(2,1)S(1)}, bf16[512,512]{1,0:T(8,128)(2,1)}, u32[]{:S(2)}) copy-start(bf16[512,512]{1,0:T(8,128)(2,1)} %param.9) | copy-start | bytes 1572868
  224.1 28.5 %all-to-all-start.1 = ((bf16[16,96,512]{2,1,0:T(8,128)(2,1)}), bf16[16,96,512]{2,1,0:T(8,128)(2,1)S(1)}, u32[]{:S(2)}, u32[]{:S(2)}) async-start(bf16[16,96,512]{2,1,0:T(8,128)(2,1)} %bitcast.36), calls=%async_computation.1 | async-start | bytes 3145728 | tf_op jit(solution)/shard_map/all_to_all | solution.py:54
  231.3 220.3 %reduce-scatter.2.cloned.1.call-start = ((), (), s32[]{:S(2)}) async-start(), calls=%async_computation.5 | async-start | bytes 8912896 | tf_op jit(solution)/shard_map/reduce_scatter | solution.py:72
  271.2 0.7 copy-start.8
  271.2 214.9 %copy-start.6 = (bf16[512,512]{1,0:T(8,128)(2,1)S(1)}, bf16[512,512]{1,0:T(8,128)(2,1)}, u32[]{:S(2)}) copy-start(bf16[512,512]{1,0:T(8,128)(2,1)} %param.12) | copy-start | bytes 1572868
  271.3 432.5 %all-reduce.9.cloned.1.call-start = ((), (), s32[]{:S(2)}) async-start(), calls=%async_computation.6 | async-start | bytes 917504 | tf_op jit(solution)/shard_map/psum | solution.py:104
  563.4 4.8 copy-start.7
  703.7 8.1 %copy-start.1 = (bf16[16,64,512]{2,1,0:T(8,128)(2,1)S(1)}, bf16[16,64,512]{2,1,0:T(8,128)(2,1)}, u32[]{:S(2)}) copy-start(bf16[16,64,512]{2,1,0:T(8,128)(2,1)} %param.13) | copy-start | bytes 3145732
Sparse Core Ops, SparseCore 0:
  62.1 137.5 all-reduce.6
  271.4 180.1 reduce-scatter.1
  568.3 135.3 all-reduce.8
where the time goes:
time: 719 us; the launch traced here: 718 us
  waiting for transfers between devices  473 us (66%)
  blocking collectives  91 us (13%)
  local copies, waits for them, and re-layouts  71 us (10%)
  matrix products  37.9 us (5%)
  other arithmetic  16.4 us (2%)
  starting transfers between devices  15.1 us (2%)
  between operations  13.9 us (2%)
    reduce_scatter x1, waiting for transfers between devices, body(): lax.psum_scatter(partial_value.astype(jnp.bfloat16), 'tensor', scatter_di...  180 us
    psum x1, waiting for transfers between devices, body(): rank_act = lax.psum(rank_part.astype(jnp.bfloat16), 'tensor')  137 us
    psum x1, waiting for transfers between devices, body(): back_act = lax.psum(back_part.astype(jnp.bfloat16), 'tensor')  128 us
    psum x1, blocking collectives, body(): square_total = lax.psum(jnp.sum(hidden * hidden, axis=1), 'tensor')  33.3 us
    gather x4, local copies, waits for them, and re-layouts, to_padded(): return extended[positions]  32.3 us
    psum x1, blocking collectives, body(): grad_total = lax.psum(jnp.sum(weighted * scaled, axis=1), 'tensor')  30.6 us
    all_to_all x1, blocking collectives, body(): lax.all_to_all(grad_send, 'dp', split_axis=0, concat_axis=0, tiled=True)  27 us
    all_to_all x1, waiting for transfers between devices, body(): lax.all_to_all(outgoing, 'dp', split_axis=0, concat_axis=0, tiled=True)  19.2 us
  transfers between devices with their start and end apart: 5, of which 5 were waited for; matrix products, arithmetic and copies ran while one was open for 3% of the time, Pallas kernels for 0%

commit v1 on v0

--- a/solution.py
+++ b/solution.py
@@ -41,7 +41,7 @@
     rank_part = jnp.einsum(
         "brk,bpk->brp", down_weight_tiles, feat_padded, preferred_element_type=jnp.float32
     )
-    rank_act = lax.psum(rank_part.astype(jnp.bfloat16), "tensor")
+    rank_act = jnp.sum(lax.all_gather(rank_part.astype(jnp.bfloat16), "tensor"), axis=0)
     delta_pad = (
         2.0
         * jnp.einsum("brp,bro->bpo", rank_act, up_weight_tiles, preferred_element_type=jnp.float32)

time: 719 us -> 747 us (1.039)
  waiting for transfers between devices: 473 us -> 500 us
    all_gather x0 -> x1, waiting for transfers between devices: none -> 162 us  [body(): lax.all_gather(rank_part.astype(jnp.bfloat16), 'tensor')]
    psum x1 -> x0, waiting for transfers between devices: 137 us -> none  [body(): rank_act = lax.psum(rank_part.astype(jnp.bfloat16), 'tensor')]
where the time goes in v1:
time: 747 us
  waiting for transfers between devices  500 us (67%)
  blocking collectives  91 us (12%)
  local copies, waits for them, and re-layouts  68.8 us (9%)
  matrix products  36.7 us (5%)
  other arithmetic  21.2 us (3%)
  starting transfers between devices  15.2 us (2%)
  between operations  13.9 us (2%)
    reduce_scatter x1, waiting for transfers between devices, body(): lax.psum_scatter(partial_value.astype(jnp.bfloat16), 'tensor', scatter_di...  181 us
    all_gather x1, waiting for transfers between devices, body(): lax.all_gather(rank_part.astype(jnp.bfloat16), 'tensor')  162 us
    psum x1, waiting for transfers between devices, body(): back_act = lax.psum(back_part.astype(jnp.bfloat16), 'tensor')  128 us
    psum x1, blocking collectives, body(): square_total = lax.psum(jnp.sum(hidden * hidden, axis=1), 'tensor')  33.3 us
    gather x4, local copies, waits for them, and re-layouts, to_padded(): return extended[positions]  32.3 us
    psum x1, blocking collectives, body(): grad_total = lax.psum(jnp.sum(weighted * scaled, axis=1), 'tensor')  30.6 us
    all_to_all x1, blocking collectives, body(): lax.all_to_all(grad_send, 'dp', split_axis=0, concat_axis=0, tiled=True)  27 us
    all_to_all x1, waiting for transfers between devices, body(): lax.all_to_all(outgoing, 'dp', split_axis=0, concat_axis=0, tiled=True)  19.2 us
  transfers between devices with their start and end apart: 5, of which 5 were waited for; matrix products, arithmetic and copies ran while one was open for 3% of the time, Pallas kernels for 0%

profile of v1, /device:TPU:2, one launch (start us, length us, event | category | flops | bytes accessed | tf_op | source)
XLA Modules:
  0.0 746.7 jit_solution(1496612492804492220)
XLA Ops:
  9.2 5.4 gather_fusion.1
  14.6 7.6 %all-to-all-start = ((bf16[16,96,512]{2,1,0:T(8,128)(2,1)}), bf16[16,96,512]{2,1,0:T(8,128)(2,1)S(1)}, u32[]{:S(2)}, u32[]{:S(2)}) async-start(bf16[16,96,512]{2,1,0:T(8,128)(2,1)} %bitcast.3), calls=%async_computation | async-start | bytes 3145728 | tf_op jit(solution)/shard_map/all_to_all | solution.py:35
  24.3 19.2 %all-to-all-done = bf16[16,96,512]{2,1,0:T(8,128)(2,1)S(1)} async-done(((bf16[16,96,512]{2,1,0:T(8,128)(2,1)}), bf16[16,96,512]{2,1,0:T(8,128)(2,1)S(1)}, u32[]{:S(2)}, u32[]{:S(2)}) %all-to-all-start) | async-done | bytes 1572896 | tf_op jit(solution)/shard_map/all_to_all | solution.py:35
  46.2 11.0 %gather_fusion.2 = bf16[3584,512]{1,0:T(8,128)(2,1)} fusion(bf16[1537,512]{1,0:T(8,128)(2,1)S(1)} %concatenate.13, s32[4096]{0:T(1024)S(1)} %pad_clamp_fusion), kind=kCustom, calls=%fused_computation.2 | custom fusion | bytes 7354368 | tf_op jit(solution)/shard_map/gather | solution.py:11
  57.2 4.8 convolution_convert_fusion
  62.7 162.3 %all-gather.3.cloned.1.call-done = bf16[448,64,128]{2,1,0:T(8,128)(2,1)} async-done(((bf16[28,64,128]{2,1,0:T(8,128)(2,1)}), bf16[448,64,128]{2,1,0:T(8,128)(2,1)}) %all-gather.3.cloned.1.call-update) | async-done | bytes 7340048 | tf_op jit(solution)/shard_map/all_gather | solution.py:44
  225.0 4.9 reduce_sum.30
  229.9 3.0 multiply_convert_fusion
  232.9 16.8 %scatter_custom_fusion = bf16[1537,512]{1,0:T(8,128)(2,1)S(1)} fusion(s32[3584]{0:T(1024)S(1)} %fusion.26, bf16[3584,512]{1,0:T(8,128)(2,1)} %bitcast.42, bf16[]{:T(256)} %constant.17.clone.1), kind=kCustom, calls=%fused_computation.33 | custom fusion | bytes 1574400 | tf_op jit(solution)/shard_map/scatter | solution.py:52
  251.0 7.3 all-to-all-start.1
  258.5 11.5 %fusion.34 = f32[512,8192]{1,0:T(8,128)} fusion(bf16[512,512]{1,0:T(8,128)(2,1)S(1)} %copy-done.4, bf16[512,8192]{1,0:T(8,128)(2,1)} %param.10), kind=kOutput, calls=%fused_computation.53 | convolution fusion | flops 4294967296 | bytes 25690112 | tf_op jit(solution)/shard_map/dot_general | solution.py:67
  270.0 9.6 %all-to-all-done.1 = bf16[16,96,512]{2,1,0:T(8,128)(2,1)S(1)} async-done(((bf16[16,96,512]{2,1,0:T(8,128)(2,1)}), bf16[16,96,512]{2,1,0:T(8,128)(2,1)S(1)}, u32[]{:S(2)}, u32[]{:S(2)}) %all-to-all-start.1) | async-done | bytes 1572896 | tf_op jit(solution)/shard_map/all_to_all | solution.py:54
  279.6 7.3 scatter_custom_fusion.1
  289.3 8.9 %convert_element_type.39 = bf16[512,8192]{1,0:T(8,128)(2,1)} convert(f32[512,8192]{1,0:T(8,128)} %add_dynamic-update-slice_fusion) | non-fusion elementwise | flops 4194304 | bytes 25165824 | tf_op jit(solution)/shard_map/convert_element_type | solution.py:73
  298.9 181.1 %reduce-scatter.2.cloned.1.call-done = bf16[512,512]{1,0:T(8,128)(2,1)} async-done(((bf16[512,8192]{1,0:T(8,128)(2,1)}), bf16[512,512]{1,0:T(8,128)(2,1)}) %reduce-scatter.2.cloned.1.call-update) | async-done | bytes 524304 | tf_op jit(solution)/shard_map/reduce_scatter | solution.py:72
  481.2 33.3 %psum.21 = f32[512]{0:T(512)S(1)} all-reduce(f32[512]{0:T(512)S(1)} %fusion.21), channel_id=1, replica_groups=mesh['dp'=16,'tensor'=16] {'tensor'}, use_global_device_ids=true, to_apply=%region_5.0 | all-reduce | flops 512 | bytes 4096 | tf_op jit(solution)/shard_map/psum | solution.py:75
  516.0 30.6 %psum.22 = f32[512]{0:T(512)S(1)} all-reduce(f32[512]{0:T(512)S(1)} %fusion.17), channel_id=1, replica_groups=mesh['dp'=16,'tensor'=16] {'tensor'}, use_global_device_ids=true, to_apply=%region_7.0 | all-reduce | flops 512 | bytes 4096 | tf_op jit(solution)/shard_map/psum | solution.py:82
  548.9 4.8 gather_fusion.4
  553.7 27.0 %all_to_all.15 = bf16[16,96,512]{2,1,0:T(8,128)(2,1)S(1)} all-to-all(bf16[16,96,512]{2,1,0:T(8,128)(2,1)S(1)} %bitcast.39), channel_id=1, replica_groups=mesh['dp'=16,'tensor'=16] {'dp'}, dimensions={0} | all-to-all | bytes 3145728 | tf_op jit(solution)/shard_map/all_to_all | solution.py:87
  580.8 11.0 %gather_fusion.5 = bf16[3584,512]{1,0:T(8,128)(2,1)} fusion(bf16[1537,512]{1,0:T(8,128)(2,1)S(1)} %concatenate.15, s32[4096]{0:T(1024)S(1)} %pad_clamp_fusion), kind=kCustom, calls=%fused_computation.5 | custom fusion | bytes 7354368 | tf_op jit(solution)/shard_map/gather | solution.py:11
  591.8 4.7 fusion.13
  599.2 3.6 fusion.7
  604.4 127.7 %all-reduce.6.cloned.1.call-done = bf16[28,64,128]{2,1,0:T(8,128)(2,1)} async-done(((bf16[28,64,128]{2,1,0:T(8,128)(2,1)}), bf16[28,64,128]{2,1,0:T(8,128)(2,1)}) %all-reduce.6.cloned.1.call-update) | async-done | bytes 458768 | tf_op jit(solution)/shard_map/psum | solution.py:104
  735.0 3.6 fusion.4
  (51 shorter events, 25.7 us)
Async XLA Ops:
  7.2 15.2 %copy-start = (bf16[16,64,512]{2,1,0:T(8,128)(2,1)S(1)}, bf16[16,64,512]{2,1,0:T(8,128)(2,1)}, u32[]{:S(2)}) copy-start(bf16[16,64,512]{2,1,0:T(8,128)(2,1)} %param.13) | copy-start | bytes 3145732
  9.2 13.1 %copy-start.9 = (s32[1,28]{1,0:T(1,128)S(1)}, s32[1,28]{1,0:T(1,128)}, u32[]{:S(2)}) copy-start(s32[1,28]{1,0:T(1,128)} %param.17) | copy-start | bytes 340
  14.6 9.7 %copy-start.8 = (s32[1,3584]{1,0:T(1,128)S(1)}, s32[1,3584]{1,0:T(1,128)}, u32[]{:S(2)}) copy-start(s32[1,3584]{1,0:T(1,128)} %param.16) | copy-start | bytes 43012
  14.6 28.9 %all-to-all-start = ((bf16[16,96,512]{2,1,0:T(8,128)(2,1)}), bf16[16,96,512]{2,1,0:T(8,128)(2,1)S(1)}, u32[]{:S(2)}, u32[]{:S(2)}) async-start(bf16[16,96,512]{2,1,0:T(8,128)(2,1)} %bitcast.3), calls=%async_computation | async-start | bytes 3145728 | tf_op jit(solution)/shard_map/all_to_all | solution.py:35
  22.2 202.8 %all-gather.3.cloned.1.call-start = ((), (), s32[]{:S(2)}) async-start(), calls=%async_computation.6 | async-start | bytes 7798784 | tf_op jit(solution)/shard_map/all_gather | solution.py:44
  43.5 1.1 copy-start.3
  57.2 4.8 copy-start.5
  62.7 167.2 %copy-start.2 = (bf16[28,64,512]{2,1,0:T(8,128)(2,1)}, bf16[28,64,512]{2,1,0:T(8,128)(2,1)S(1)}, u32[]{:S(2)}) copy-start(bf16[28,64,512]{2,1,0:T(8,128)(2,1)S(1)} %gather_fusion.3) | copy-start | bytes 5505028
  232.9 25.6 %copy-start.4 = (bf16[512,512]{1,0:T(8,128)(2,1)S(1)}, bf16[512,512]{1,0:T(8,128)(2,1)}, u32[]{:S(2)}) copy-start(bf16[512,512]{1,0:T(8,128)(2,1)} %param.9) | copy-start | bytes 1572868
  251.0 28.6 %all-to-all-start.1 = ((bf16[16,96,512]{2,1,0:T(8,128)(2,1)}), bf16[16,96,512]{2,1,0:T(8,128)(2,1)S(1)}, u32[]{:S(2)}, u32[]{:S(2)}) async-start(bf16[16,96,512]{2,1,0:T(8,128)(2,1)} %bitcast.38), calls=%async_computation.1 | async-start | bytes 3145728 | tf_op jit(solution)/shard_map/all_to_all | solution.py:54
  258.3 221.7 %reduce-scatter.2.cloned.1.call-start = ((), (), s32[]{:S(2)}) async-start(), calls=%async_computation.4 | async-start | bytes 8912896 | tf_op jit(solution)/shard_map/reduce_scatter | solution.py:72
  298.2 0.7 copy-start.7
  298.2 216.3 %copy-start.6 = (bf16[512,512]{1,0:T(8,128)(2,1)S(1)}, bf16[512,512]{1,0:T(8,128)(2,1)}, u32[]{:S(2)}) copy-start(bf16[512,512]{1,0:T(8,128)(2,1)} %param.12) | copy-start | bytes 1572868
  298.2 433.9 %all-reduce.6.cloned.1.call-start = ((), (), s32[]{:S(2)}) async-start(), calls=%async_computation.5 | async-start | bytes 917504 | tf_op jit(solution)/shard_map/psum | solution.py:104
  732.1 8.1 %copy-start.1 = (bf16[16,64,512]{2,1,0:T(8,128)(2,1)S(1)}, bf16[16,64,512]{2,1,0:T(8,128)(2,1)}, u32[]{:S(2)}) copy-start(bf16[16,64,512]{2,1,0:T(8,128)(2,1)} %param.13) | copy-start | bytes 3145732
Sparse Core Ops, SparseCore 0:
  62.1 162.8 all-gather.2
  298.4 181.5 reduce-scatter.1
  596.7 135.3 all-reduce.5
